TPU v7x, 32 devices: a whole 2x2x4 slice. The times are simulated.
32 devices in a mesh: group: 2 (over y), expert: 4 (over z), query: 2 (over x), dp: 2 (over core).
Axes of the slice: x: 2, y: 2, z: 4, core: 2. Of those that a mesh axis runs over, the one named last changes fastest.
Arguments:
- tokens: bfloat16 [4096, 2048], P(('group', 'expert', 'query', 'dp')), parts along dimension 0, may hold values from -6 to 6
- route_ids: int32 [4096, 4], P(('group', 'expert', 'query', 'dp')), parts along dimension 0, may hold values from 0 to 7, all different within a row; in each aligned block of 128 rows (0 to 127, 128 to 255, ...) at most 128 rows name the same one
- gate_values: float32 [4096, 4], P(('group', 'expert', 'query', 'dp')), parts along dimension 0, may hold values from 0.1 to 1
- passage_lengths: int32 [64], P(('group', 'expert', 'query', 'dp')), parts along dimension 0, may hold values from 16 to 64
- gate_weight: bfloat16 [8, 2048, 384], P(('expert', 'query'), None, 'dp'), may hold values from -0.125 to 0.125
- up_weight: bfloat16 [8, 2048, 384], P(('expert', 'query'), None, 'dp'), may hold values from -0.125 to 0.125
- down_weight: bfloat16 [8, 2048, 384], P(('expert', 'query'), None, 'dp'), may hold values from -0.3125 to 0.3125
- proj_weight: bfloat16 [2048, 128], replicated, may hold values from -0.125 to 0.125
- queries: bfloat16 [128, 32, 128], P(('group', 'query')), parts along dimension 0, may hold values from -0.59765625 to 0.59765625
Outputs:
- scores: float32 [64, 64], P(('group', 'expert', 'query', 'dp')), parts along dimension 0
There are 2 independent parts, one for each index of `group`. A program takes and returns all parts, laid end to end along the dimension named above; an argument that names none is the same for every part. Nothing has to cross between parts.
Inputs may be any that keep to these rules, and one draw needn't show every extreme that they name: `route_ids`: in the rows of one device no expert is named more than 128 times, a bound that some block reaches.
All inputs are finite; a program needn't handle non-finite values.
Results may differ from a plain program's by a relative error of at most 0.0006.
Values may be sent and summed in bfloat16 or wider, within the bound.
A program may use at most 64 MiB of HBM per device.

v0:
```python
import jax
import jax.numpy as jnp
from jax import lax
from jax.sharding import PartitionSpec as P

PLEN = 64


def passage_scores(embedding, live_mask, block_queries):
    query_rows = block_queries.reshape(-1, block_queries.shape[-1])
    raw_scores = jnp.dot(embedding, query_rows.T, preferred_element_type=jnp.float32)
    raw_scores = jnp.where(live_mask[:, None], raw_scores, -jnp.inf)
    best_match = jnp.max(raw_scores.reshape(-1, PLEN, raw_scores.shape[-1]), axis=1)
    return jnp.sum(best_match.reshape(best_match.shape[0], -1, block_queries.shape[1]), axis=-1)


def on_device(
    tokens,
    route_ids,
    gate_values,
    passage_lengths,
    gate_weight,
    up_weight,
    down_weight,
    proj_weight,
    queries,
):
    tok_rows, model_width = tokens.shape
    top_count = route_ids.shape[1]
    experts = lax.axis_size("expert") * lax.axis_size("query")
    capacity = max(2, 2 * tok_rows * top_count // experts)
    assignments = tok_rows * top_count
    flat_routes = route_ids.reshape(-1)
    one_hot = (flat_routes[:, None] == jnp.arange(experts, dtype=jnp.int32)[None, :]).astype(
        jnp.int32
    )
    earlier = jnp.cumsum(one_hot, axis=0) - one_hot
    slot_index = jnp.sum(earlier * one_hot, axis=1)
    slot_target = flat_routes * capacity + slot_index
    slot_owner = (
        jnp.full((experts * capacity,), assignments, jnp.int32)
        .at[slot_target]
        .set(jnp.arange(assignments, dtype=jnp.int32))
    )
    padded = jnp.concatenate([tokens, jnp.zeros((1, model_width), tokens.dtype)], axis=0)
    source_row = jnp.where(slot_owner < assignments, slot_owner // top_count, tok_rows)
    outgoing = padded[source_row].reshape(experts, capacity, model_width)
    arrived = lax.all_to_all(outgoing, ("expert", "query"), split_axis=0, concat_axis=0, tiled=True)
    expert_rows = arrived.reshape(experts * capacity, model_width)
    gate_act = jnp.dot(
        expert_rows,
        lax.all_gather(gate_weight[0], "dp", axis=1, tiled=True),
        preferred_element_type=jnp.float32,
    )
    up_act = jnp.dot(
        expert_rows,
        lax.all_gather(up_weight[0], "dp", axis=1, tiled=True),
        preferred_element_type=jnp.float32,
    )
    hidden = (jax.nn.silu(gate_act) * up_act).astype(jnp.bfloat16)
    accumulated = lax.dot_general(
        hidden,
        lax.all_gather(down_weight[0], "dp", axis=1, tiled=True),
        (((1,), (1,)), ((), ())),
        preferred_element_type=jnp.float32,
    )
    results = accumulated.astype(jnp.bfloat16)
    weights = gate_values.reshape(assignments, 1)
    folded = jnp.dot(results, proj_weight, preferred_element_type=jnp.float32)
    returned_rows = lax.all_to_all(
        folded.reshape(experts, capacity, folded.shape[-1]),
        ("expert", "query"),
        split_axis=0,
        concat_axis=0,
        tiled=True,
    )
    picked = returned_rows.reshape(experts * capacity, folded.shape[-1])[slot_target]
    projected = jnp.dot(tokens, proj_weight, preferred_element_type=jnp.float32) + jnp.sum(
        (picked * weights).reshape(tok_rows, top_count, folded.shape[-1]), axis=1
    )
    lengths_norm = jnp.sqrt(jnp.sum(projected * projected, axis=-1, keepdims=True) + 1e-06)
    embedding = (projected / lengths_norm).astype(jnp.bfloat16)
    position = jnp.arange(tok_rows, dtype=jnp.int32) % PLEN
    live_mask = position < jnp.repeat(passage_lengths, PLEN)
    return passage_scores(
        embedding, live_mask, lax.all_gather(queries, "query", axis=0, tiled=True)
    )


def solution(mesh):
    in_specs = (
        P(("group", "expert", "query", "dp"), None),
        P(("group", "expert", "query", "dp"), None),
        P(("group", "expert", "query", "dp"), None),
        P(("group", "expert", "query", "dp")),
        P(("expert", "query"), None, "dp"),
        P(("expert", "query"), None, "dp"),
        P(("expert", "query"), None, "dp"),
        P(),
        P(("group", "query"), None, None),
    )
    out_specs = P(("group", "expert", "query", "dp"), None)
    return jax.shard_map(
        on_device, mesh=mesh, in_specs=in_specs, out_specs=out_specs, check_vma=False
    )
```

profile of v0, /device:TPU:0, one launch (start us, length us, event | category | flops | bytes accessed | tf_op | source)
XLA Modules:
  0.0 163.8 jit_solution(16316723009276893319)
XLA Ops:
  6.5 0.0 copy-start
  6.5 0.8 copy.16
  7.4 0.1 eq.31
  7.5 0.1 eq.27
  7.6 0.7 broadcast_multiply_fusion
  8.3 1.1 reduce-window.6
  9.4 0.2 slice_reduce_fusion
  9.7 0.1 copy.15
  9.8 0.1 mul.40
  9.9 0.1 fusion.14
  10.0 2.4 %scatter_custom_fusion = s32[1024]{0:T(1024)S(1)} fusion(s32[512]{0:T(512)S(1)} %bitcast.41, s32[512]{0:T(512)S(1)} %iota.17, s32[]{:T(128)} %constant.46.clone.1), kind=kCustom, calls=%fused_computation.38 | custom fusion | bytes 4100 | tf_op jit(solution)/shard_map/scatter | solution.py:43
  12.5 1.1 concatenate.3
  13.6 6.0 %gather_fusion = bf16[1024,2048]{1,0:T(8,128)(2,1)} fusion(bf16[129,2048]{1,0:T(8,128)(2,1)S(1)} %concatenate.3, s32[1024]{0:T(1024)S(1)} %fusion.18), kind=kCustom, calls=%fused_computation | custom fusion | bytes 8392704 | tf_op jit(solution)/shard_map/gather | solution.py:47
  19.6 7.3 %all-to-all-start = ((bf16[8,128,2048]{2,1,0:T(8,128)(2,1)}), bf16[8,128,2048]{2,1,0:T(8,128)(2,1)}, u32[]{:S(2)}, u32[]{:S(2)}) async-start(bf16[8,128,2048]{2,1,0:T(8,128)(2,1)} %bitcast.37), calls=%async_computation | async-start | bytes 8388608 | tf_op jit(solution)/shard_map/all_to_all | solution.py:48
  26.9 0.0 all-gather.7.cloned.1.call-start
  26.9 0.7 all-gather.7.cloned.1.call-update
  27.6 0.0 all-gather.9.cloned.1.call-start
  27.7 0.7 all-gather.9.cloned.1.call-update
  28.4 0.0 all-gather.11.cloned.1.call-start
  28.4 0.7 all-gather.11.cloned.1.call-update
  29.1 11.4 %all-gather.7.cloned.1.call-done = bf16[1,2048,384]{1,2,0:T(8,128)(2,1)} async-done(((bf16[1,2048,192]{1,2,0:T(8,128)(2,1)}), bf16[1,2048,384]{1,2,0:T(8,128)(2,1)}) %all-gather.7.cloned.1.call-update) | async-done | bytes 1572880 | tf_op jit(solution)/shard_map/all_gather | solution.py:52
  40.5 79.7 %all-to-all-done = bf16[8,128,2048]{2,1,0:T(8,128)(2,1)} async-done(((bf16[8,128,2048]{2,1,0:T(8,128)(2,1)}), bf16[8,128,2048]{2,1,0:T(8,128)(2,1)}, u32[]{:S(2)}, u32[]{:S(2)}) %all-to-all-start) | async-done | bytes 4194336 | tf_op jit(solution)/shard_map/all_to_all | solution.py:48
  120.2 5.0 %fusion.8 = f32[1024,384]{1,0:T(8,128)S(1)} fusion(bf16[1024,2048]{1,0:T(8,128)(2,1)} %bitcast.5, bf16[1,2048,384]{1,2,0:T(8,128)(2,1)} %all-gather.7.cloned.1.call-done), kind=kOutput, calls=%fused_computation.10 | convolution fusion | flops 1610612736 | bytes 7340032 | tf_op jit(solution)/shard_map/dot_general | solution.py:50
  125.2 0.0 all-gather.9.cloned.1.call-done
  125.2 5.1 %multiply_convert_fusion = bf16[1024,384]{1,0:T(8,128)(2,1)S(1)} fusion(f32[1024,384]{1,0:T(8,128)S(1)} %fusion.8, bf16[1024,2048]{1,0:T(8,128)(2,1)} %bitcast.5, bf16[1,2048,384]{1,2,0:T(8,128)(2,1)} %all-gather.9.cloned.1.call-done), kind=kOutput, calls=%fused_computation.12 | convolution fusion | flops 1612972032 | bytes 8126464 | tf_op jit(solution)/shard_map/dot_general | solution.py:55
  130.4 0.0 copy-start.3
  130.4 0.0 copy-start.4
  130.4 0.0 copy-start.2
  130.4 0.0 all-gather.11.cloned.1.call-done
  130.4 0.0 copy-done
  130.4 5.7 %fusion = f32[1024,128]{1,0:T(8,128)} fusion(bf16[2048,128]{1,0:T(8,128)(2,1)S(1)} %copy-done, bf16[1024,384]{1,0:T(8,128)(2,1)S(1)} %multiply_convert_fusion, bf16[1,2048,384]{1,2,0:T(8,128)(2,1)} %all-gather.11.cloned.1.call-done), kind=kOutput, calls=%fused_computation.3 | convolution fusion | flops 2149580800 | bytes 3407872 | tf_op jit(solution)/shard_map/dot_general | solution.py:69
  136.1 3.6 %all-to-all-start.1 = ((f32[8,128,128]{2,1,0:T(8,128)}), f32[8,128,128]{2,1,0:T(8,128)S(1)}, u32[]{:S(2)}, u32[]{:S(2)}) async-start(f32[8,128,128]{2,1,0:T(8,128)} %bitcast.9), calls=%async_computation.1 | async-start | bytes 1048576 | tf_op jit(solution)/shard_map/all_to_all | solution.py:70
  139.8 0.0 copy-done.3
  139.8 0.1 copy.18
  139.9 0.0 copy-done.4
  139.9 0.1 broadcast_in_dim.28
  140.0 0.1 reshape.99
  140.0 0.0 copy-done.2
  140.1 13.5 %all_gather.15 = bf16[64,32,128]{2,1,0:T(8,128)(2,1)S(1)} all-gather(bf16[32,32,128]{2,1,0:T(8,128)(2,1)S(1)} %copy-done.2), channel_id=1, replica_groups=mesh['group'=2,'expert'=4,'query'=2,'dp'=2] {'query'}, dimensions={0}, use_global_device_ids=true | all-gather | bytes 786432 | tf_op jit(solution)/shard_map/all_gather | solution.py:86
  153.6 0.8 all-to-all-done.1
  154.4 1.0 gather_fusion.1
  155.5 0.2 multiply_reduce_fusion
  155.7 0.1 copy.19
  155.8 0.0 copy-done.1
  155.8 0.4 multiply_reduce_fusion.1
  156.2 0.4 bitcast_reduce_fusion
  156.6 0.1 reshape.107
  156.7 0.7 reduce_sum.42
  (10 shorter events, 0.1 us)
Async XLA Ops:
  6.5 123.9 %copy-start = (bf16[2048,128]{1,0:T(8,128)(2,1)S(1)}, bf16[2048,128]{1,0:T(8,128)(2,1)}, u32[]{:S(2)}) copy-start(bf16[2048,128]{1,0:T(8,128)(2,1)} %param.16) | copy-start | bytes 1572868
  19.6 100.6 %all-to-all-start = ((bf16[8,128,2048]{2,1,0:T(8,128)(2,1)}), bf16[8,128,2048]{2,1,0:T(8,128)(2,1)}, u32[]{:S(2)}, u32[]{:S(2)}) async-start(bf16[8,128,2048]{2,1,0:T(8,128)(2,1)} %bitcast.37), calls=%async_computation | async-start | bytes 8388608 | tf_op jit(solution)/shard_map/all_to_all | solution.py:48
  26.9 13.6 %all-gather.7.cloned.1.call-start = ((), (), s32[]{:S(2)}) async-start(), calls=%async_computation.2 | async-start | bytes 2359296 | tf_op jit(solution)/shard_map/all_gather | solution.py:52
  27.6 97.6 %all-gather.9.cloned.1.call-start = ((), (), s32[]{:S(2)}) async-start(), calls=%async_computation.3 | async-start | bytes 2359296 | tf_op jit(solution)/shard_map/all_gather | solution.py:57
  28.4 102.0 %all-gather.11.cloned.1.call-start = ((), (), s32[]{:S(2)}) async-start(), calls=%async_computation.4 | async-start | bytes 2359296 | tf_op jit(solution)/shard_map/all_gather | solution.py:63
  130.4 9.4 %copy-start.3 = (f32[128,4]{0,1:T(4,128)S(1)}, f32[128,4]{0,1:T(4,128)}, u32[]{:S(2)}) copy-start(f32[128,4]{0,1:T(4,128)} %param.11) | copy-start | bytes 6148
  130.4 9.5 %copy-start.4 = (s32[2]{0:T(128)S(1)}, s32[2]{0:T(128)}, u32[]{:S(2)}) copy-start(s32[2]{0:T(128)} %param.12) | copy-start | bytes 28
  130.4 9.7 %copy-start.2 = (bf16[32,32,128]{2,1,0:T(8,128)(2,1)S(1)}, bf16[32,32,128]{2,1,0:T(8,128)(2,1)}, u32[]{:S(2)}) copy-start(bf16[32,32,128]{2,1,0:T(8,128)(2,1)} %param.17) | copy-start | bytes 786436
  136.1 18.3 %all-to-all-start.1 = ((f32[8,128,128]{2,1,0:T(8,128)}), f32[8,128,128]{2,1,0:T(8,128)S(1)}, u32[]{:S(2)}, u32[]{:S(2)}) async-start(f32[8,128,128]{2,1,0:T(8,128)} %bitcast.9), calls=%async_computation.1 | async-start | bytes 1048576 | tf_op jit(solution)/shard_map/all_to_all | solution.py:70
  153.6 2.2 %copy-start.1 = (bf16[128,2048]{1,0:T(8,128)(2,1)S(1)}, bf16[128,2048]{1,0:T(8,128)(2,1)}, u32[]{:S(2)}) copy-start(bf16[128,2048]{1,0:T(8,128)(2,1)} %param.9) | copy-start | bytes 1572868
Sparse Core Ops, SparseCore 0:
  29.2 11.2 all-gather.6
  42.0 10.9 all-gather.8
  54.6 10.9 all-gather.10
where the time goes:
time: 164 us
  waiting for transfers between devices  94 us (57%)
  matrix products  16.6 us (10%)
  blocking collectives  13.5 us (8%)
  between operations  13.3 us (8%)
  local copies, waits for them, and re-layouts  12.6 us (8%)
  starting transfers between devices  11 us (7%)
  other arithmetic  2.88 us (2%)
    all_to_all x1, waiting for transfers between devices, on_device(): lax.all_to_all(outgoing, ('expert', 'query'), split_axis=0, concat_axis=0...  79.7 us
    all_gather x1, blocking collectives, on_device(): lax.all_gather(queries, 'query', axis=0, tiled=True)  13.5 us
    all_gather x1, waiting for transfers between devices, on_device(): lax.all_gather(gate_weight[0], 'dp', axis=1, tiled=True)  11.4 us
    all_to_all x1, starting transfers between devices, on_device(): lax.all_to_all(outgoing, ('expert', 'query'), split_axis=0, concat_axis=0...  7.28 us
    gather x1, local copies, waits for them, and re-layouts, on_device(): outgoing = padded[source_row].reshape(experts, capacity, model_width)  6.03 us
    dot_general x1, matrix products, on_device(): folded = jnp.dot(results, proj_weight, preferred_element_type=jnp.float32)  5.7 us
    dot_general x1, matrix products, on_device(): jnp.dot(expert_rows, lax.all_gather(up_weight[0], 'dp', axis=1, tiled=Tru...  5.12 us
    dot_general x1, matrix products, on_device(): jnp.dot(expert_rows, lax.all_gather(gate_weight[0], 'dp', axis=1, tiled=T...  5.02 us
  transfers between devices with their start and end apart: 5, of which 3 were waited for; matrix products, arithmetic and copies ran while one was open for 6% of the time, Pallas kernels for 0%

commit v1 on v0

--- a/solution.py
+++ b/solution.py
@@ -49,7 +49,7 @@
     expert_rows = arrived.reshape(experts * capacity, model_width)
     gate_act = jnp.dot(
         expert_rows,
-        lax.all_gather(gate_weight[0], "dp", axis=1, tiled=True),
+        jnp.concatenate(lax.all_gather(gate_weight[0], "dp"), axis=1),
         preferred_element_type=jnp.float32,
     )
     up_act = jnp.dot(

time: 164 us -> 164 us (level)
  no operation moved by 1% of the time
where the time goes in v1:
time: 164 us
  waiting for transfers between devices  94 us (57%)
  matrix products  16.6 us (10%)
  blocking collectives  13.5 us (8%)
  between operations  13.3 us (8%)
  local copies, waits for them, and re-layouts  12.6 us (8%)
  starting transfers between devices  11 us (7%)
  other arithmetic  2.88 us (2%)
    all_to_all x1, waiting for transfers between devices, on_device(): lax.all_to_all(outgoing, ('expert', 'query'), split_axis=0, concat_axis=0...  79.7 us
    all_gather x1, blocking collectives, on_device(): lax.all_gather(queries, 'query', axis=0, tiled=True)  13.5 us
    all_gather x1, waiting for transfers between devices, on_device(): lax.all_gather(gate_weight[0], 'dp')  11.4 us
    all_to_all x1, starting transfers between devices, on_device(): lax.all_to_all(outgoing, ('expert', 'query'), split_axis=0, concat_axis=0...  7.28 us
    gather x1, local copies, waits for them, and re-layouts, on_device(): outgoing = padded[source_row].reshape(experts, capacity, model_width)  6.03 us
    dot_general x1, matrix products, on_device(): folded = jnp.dot(results, proj_weight, preferred_element_type=jnp.float32)  5.7 us
    dot_general x1, matrix products, on_device(): jnp.dot(expert_rows, lax.all_gather(up_weight[0], 'dp', axis=1, tiled=Tru...  5.12 us
    dot_general x1, matrix products, on_device(): jnp.dot(expert_rows, jnp.concatenate(lax.all_gather(gate_weight[0], 'dp')...  5.02 us
  transfers between devices with their start and end apart: 5, of which 3 were waited for; matrix products, arithmetic and copies ran while one was open for 6% of the time, Pallas kernels for 0%

profile of v1, /device:TPU:0, one launch (start us, length us, event | category | flops | bytes accessed | tf_op | source)
XLA Modules:
  0.0 163.8 jit_solution(16316723009276893319)
XLA Ops:
  6.5 0.0 copy-start
  6.5 0.8 copy.16
  7.4 0.1 eq.31
  7.5 0.1 eq.27
  7.6 0.7 broadcast_multiply_fusion
  8.3 1.1 reduce-window.6
  9.4 0.2 slice_reduce_fusion
  9.7 0.1 copy.15
  9.8 0.1 mul.40
  9.9 0.1 fusion.12
  10.0 2.4 %scatter_custom_fusion = s32[1024]{0:T(1024)S(1)} fusion(s32[512]{0:T(512)S(1)} %bitcast.42, s32[512]{0:T(512)S(1)} %iota.17, s32[]{:T(128)} %constant.46.clone.1), kind=kCustom, calls=%fused_computation.36 | custom fusion | bytes 4100 | tf_op jit(solution)/shard_map/scatter | solution.py:43
  12.5 1.1 concatenate.3
  13.6 6.0 %gather_fusion = bf16[1024,2048]{1,0:T(8,128)(2,1)} fusion(bf16[129,2048]{1,0:T(8,128)(2,1)S(1)} %concatenate.3, s32[1024]{0:T(1024)S(1)} %fusion.16), kind=kCustom, calls=%fused_computation | custom fusion | bytes 8392704 | tf_op jit(solution)/shard_map/gather | solution.py:47
  19.6 7.3 %all-to-all-start = ((bf16[8,128,2048]{2,1,0:T(8,128)(2,1)}), bf16[8,128,2048]{2,1,0:T(8,128)(2,1)}, u32[]{:S(2)}, u32[]{:S(2)}) async-start(bf16[8,128,2048]{2,1,0:T(8,128)(2,1)} %bitcast.38), calls=%async_computation | async-start | bytes 8388608 | tf_op jit(solution)/shard_map/all_to_all | solution.py:48
  26.9 0.0 all-gather.6.cloned.1.call-start
  26.9 0.7 all-gather.6.cloned.1.call-update
  27.6 0.0 all-gather.8.cloned.1.call-start
  27.7 0.7 all-gather.8.cloned.1.call-update
  28.4 0.0 all-gather.10.cloned.1.call-start
  28.4 0.7 all-gather.10.cloned.1.call-update
  29.1 11.4 %all-gather.6.cloned.1.call-done = bf16[2,2048,192]{1,2,0:T(8,128)(2,1)} async-done(((bf16[1,2048,192]{1,2,0:T(8,128)(2,1)}), bf16[2,2048,192]{1,2,0:T(8,128)(2,1)}) %all-gather.6.cloned.1.call-update) | async-done | bytes 1572880 | tf_op jit(solution)/shard_map/all_gather | solution.py:52
  40.5 79.7 %all-to-all-done = bf16[8,128,2048]{2,1,0:T(8,128)(2,1)} async-done(((bf16[8,128,2048]{2,1,0:T(8,128)(2,1)}), bf16[8,128,2048]{2,1,0:T(8,128)(2,1)}, u32[]{:S(2)}, u32[]{:S(2)}) %all-to-all-start) | async-done | bytes 4194336 | tf_op jit(solution)/shard_map/all_to_all | solution.py:48
  120.2 5.0 %fusion.21 = f32[1024,384]{1,0:T(8,128)S(1)} fusion(bf16[1024,2048]{1,0:T(8,128)(2,1)} %bitcast.5, bf16[2048,384]{0,1:T(8,128)(2,1)} %bitcast.45), kind=kOutput, calls=%fused_computation.42 | convolution fusion | flops 1610612736 | bytes 7340032 | tf_op jit(solution)/shard_map/dot_general | solution.py:50
  125.2 0.0 all-gather.8.cloned.1.call-done
  125.2 5.1 %multiply_convert_fusion = bf16[1024,384]{1,0:T(8,128)(2,1)S(1)} fusion(f32[1024,384]{1,0:T(8,128)S(1)} %fusion.21, bf16[1024,2048]{1,0:T(8,128)(2,1)} %bitcast.5, bf16[1,2048,384]{1,2,0:T(8,128)(2,1)} %all-gather.8.cloned.1.call-done), kind=kOutput, calls=%fused_computation.10 | convolution fusion | flops 1612972032 | bytes 8126464 | tf_op jit(solution)/shard_map/dot_general | solution.py:55
  130.4 0.0 copy-start.3
  130.4 0.0 copy-start.4
  130.4 0.0 copy-start.2
  130.4 0.0 all-gather.10.cloned.1.call-done
  130.4 0.0 copy-done
  130.4 5.7 %fusion = f32[1024,128]{1,0:T(8,128)} fusion(bf16[2048,128]{1,0:T(8,128)(2,1)S(1)} %copy-done, bf16[1024,384]{1,0:T(8,128)(2,1)S(1)} %multiply_convert_fusion, bf16[1,2048,384]{1,2,0:T(8,128)(2,1)} %all-gather.10.cloned.1.call-done), kind=kOutput, calls=%fused_computation.3 | convolution fusion | flops 2149580800 | bytes 3407872 | tf_op jit(solution)/shard_map/dot_general | solution.py:69
  136.1 3.6 %all-to-all-start.1 = ((f32[8,128,128]{2,1,0:T(8,128)}), f32[8,128,128]{2,1,0:T(8,128)S(1)}, u32[]{:S(2)}, u32[]{:S(2)}) async-start(f32[8,128,128]{2,1,0:T(8,128)} %bitcast.10), calls=%async_computation.1 | async-start | bytes 1048576 | tf_op jit(solution)/shard_map/all_to_all | solution.py:70
  139.8 0.0 copy-done.3
  139.8 0.1 copy.18
  139.9 0.0 copy-done.4
  139.9 0.1 broadcast_in_dim.28
  140.0 0.1 reshape.105
  140.0 0.0 copy-done.2
  140.1 13.5 %all_gather.15 = bf16[64,32,128]{2,1,0:T(8,128)(2,1)S(1)} all-gather(bf16[32,32,128]{2,1,0:T(8,128)(2,1)S(1)} %copy-done.2), channel_id=1, replica_groups=mesh['group'=2,'expert'=4,'query'=2,'dp'=2] {'query'}, dimensions={0}, use_global_device_ids=true | all-gather | bytes 786432 | tf_op jit(solution)/shard_map/all_gather | solution.py:86
  153.6 0.8 all-to-all-done.1
  154.4 1.0 gather_fusion.1
  155.5 0.2 multiply_reduce_fusion
  155.7 0.1 copy.19
  155.8 0.0 copy-done.1
  155.8 0.4 multiply_reduce_fusion.1
  156.2 0.4 bitcast_reduce_fusion
  156.6 0.1 reshape.115
  156.7 0.7 reduce_sum.42
  (10 shorter events, 0.1 us)
Async XLA Ops:
  6.5 123.9 %copy-start = (bf16[2048,128]{1,0:T(8,128)(2,1)S(1)}, bf16[2048,128]{1,0:T(8,128)(2,1)}, u32[]{:S(2)}) copy-start(bf16[2048,128]{1,0:T(8,128)(2,1)} %param.16) | copy-start | bytes 1572868
  19.6 100.6 %all-to-all-start = ((bf16[8,128,2048]{2,1,0:T(8,128)(2,1)}), bf16[8,128,2048]{2,1,0:T(8,128)(2,1)}, u32[]{:S(2)}, u32[]{:S(2)}) async-start(bf16[8,128,2048]{2,1,0:T(8,128)(2,1)} %bitcast.38), calls=%async_computation | async-start | bytes 8388608 | tf_op jit(solution)/shard_map/all_to_all | solution.py:48
  26.9 13.6 %all-gather.6.cloned.1.call-start = ((), (), s32[]{:S(2)}) async-start(), calls=%async_computation.2 | async-start | bytes 2359296 | tf_op jit(solution)/shard_map/all_gather | solution.py:52
  27.6 97.6 %all-gather.8.cloned.1.call-start = ((), (), s32[]{:S(2)}) async-start(), calls=%async_computation.3 | async-start | bytes 2359296 | tf_op jit(solution)/shard_map/all_gather | solution.py:57
  28.4 102.0 %all-gather.10.cloned.1.call-start = ((), (), s32[]{:S(2)}) async-start(), calls=%async_computation.4 | async-start | bytes 2359296 | tf_op jit(solution)/shard_map/all_gather | solution.py:63
  130.4 9.4 %copy-start.3 = (f32[128,4]{0,1:T(4,128)S(1)}, f32[128,4]{0,1:T(4,128)}, u32[]{:S(2)}) copy-start(f32[128,4]{0,1:T(4,128)} %param.11) | copy-start | bytes 6148
  130.4 9.5 %copy-start.4 = (s32[2]{0:T(128)S(1)}, s32[2]{0:T(128)}, u32[]{:S(2)}) copy-start(s32[2]{0:T(128)} %param.12) | copy-start | bytes 28
  130.4 9.7 %copy-start.2 = (bf16[32,32,128]{2,1,0:T(8,128)(2,1)S(1)}, bf16[32,32,128]{2,1,0:T(8,128)(2,1)}, u32[]{:S(2)}) copy-start(bf16[32,32,128]{2,1,0:T(8,128)(2,1)} %param.17) | copy-start | bytes 786436
  136.1 18.3 %all-to-all-start.1 = ((f32[8,128,128]{2,1,0:T(8,128)}), f32[8,128,128]{2,1,0:T(8,128)S(1)}, u32[]{:S(2)}, u32[]{:S(2)}) async-start(f32[8,128,128]{2,1,0:T(8,128)} %bitcast.10), calls=%async_computation.1 | async-start | bytes 1048576 | tf_op jit(solution)/shard_map/all_to_all | solution.py:70
  153.6 2.2 %copy-start.1 = (bf16[128,2048]{1,0:T(8,128)(2,1)S(1)}, bf16[128,2048]{1,0:T(8,128)(2,1)}, u32[]{:S(2)}) copy-start(bf16[128,2048]{1,0:T(8,128)(2,1)} %param.9) | copy-start | bytes 1572868
Sparse Core Ops, SparseCore 0:
  29.2 11.2 all-gather.5
  42.0 10.9 all-gather.7
  54.6 10.9 all-gather.9
